TPU v7x, 256 devices: a whole 4x4x8 slice. The times are simulated.
256 devices in a mesh: feat: 64 (over z_lo, y, x), tgt: 4 (over z_hi, core).
Axes of the slice: x: 4, y: 4, z: 8 (z_hi: 2, z_lo: 4; z = z_hi * 4 + z_lo), core: 2. Of those that a mesh axis runs over, the one named last changes fastest.
Arguments:
- tokens: bfloat16 [192, 4096], P('feat'), may hold values from -6 to 6
- encoder_weight: bfloat16 [4096, 16384], P(None, 'feat'), may hold values from -0.09375 to 0.09375
- encoder_bias: float32 [16384], P('feat'), may hold values from -1 to 0.25
- decoder_weight: bfloat16 [4, 16384, 4096], P('tgt', 'feat'), may hold values from -0.046875 to 0.046875
- decoder_bias: float32 [4, 4096], P('tgt'), may hold values from -3 to 3
- targets: bfloat16 [4, 192, 4096], P('tgt', 'feat'), may hold values from -6 to 6
Outputs:
- encoder_grad: float32 [4096, 16384], P(None, ('feat', 'tgt'))
- encoder_bias_grad: float32 [16384], P(('feat', 'tgt'))
- decoder_grad: float32 [4, 16384, 4096], P('tgt', 'feat')
- decoder_bias_grad: float32 [4, 4096], P('tgt')
All inputs are finite; a program needn't handle non-finite values.
Results may differ from a plain program's by a relative error of at most 0.005.
Values may be sent and summed in bfloat16 or wider, within the bound.
No kernel may reach another device: no remote copies, remote signals or barrier semaphores. Data moves between devices by JAX's collectives and lax.ppermute only.
A program may use at most 64 MiB of HBM per device.

v0:
```python
import jax
import jax.numpy as jnp
from jax import lax
from jax.sharding import PartitionSpec as P


def body(tokens, encoder_weight, encoder_bias, decoder_weight, decoder_bias, targets):
    all_rows = lax.all_gather(tokens, "feat", axis=0, tiled=True)
    pre_act = jnp.dot(all_rows, encoder_weight, preferred_element_type=jnp.float32) + encoder_bias
    positive = jnp.maximum(pre_act, 0.0)
    feats = (positive**2).astype(jnp.bfloat16)
    weight = decoder_weight[0]
    bias = decoder_bias[0]
    target = targets[0]
    summed = lax.psum_scatter(
        jnp.dot(feats, weight, preferred_element_type=jnp.float32),
        "feat",
        scatter_dimension=0,
        tiled=True,
    )
    error_part = (summed + bias - target.astype(jnp.float32)).astype(jnp.bfloat16)
    recon_error = lax.all_gather(error_part, "feat", axis=0, tiled=True)
    decoder_grads = [
        lax.dot_general(
            feats, recon_error, (((0,), (0,)), ((), ())), preferred_element_type=jnp.float32
        )
    ]
    bias_grads = [jnp.sum(recon_error.astype(jnp.float32), axis=0)]
    back_grad = lax.dot_general(
        recon_error, weight, (((1,), (1,)), ((), ())), preferred_element_type=jnp.float32
    )
    quarter = pre_act.shape[1] // lax.axis_size("tgt")
    offset = lax.axis_index("tgt") * quarter
    share = lax.psum_scatter(back_grad, "tgt", scatter_dimension=1, tiled=True)
    slope_share = 2.0 * lax.dynamic_slice_in_dim(positive, offset, quarter, 1)
    act_grad = share * slope_share
    encoder_bias_grad = jnp.sum(act_grad, axis=0)
    pre_grad = act_grad.astype(jnp.bfloat16)
    encoder_grad = lax.dot_general(
        all_rows, pre_grad, (((0,), (0,)), ((), ())), preferred_element_type=jnp.float32
    )
    return (encoder_grad, encoder_bias_grad, jnp.stack(decoder_grads), jnp.stack(bias_grads))


def solution(mesh):
    return jax.shard_map(
        body,
        mesh=mesh,
        in_specs=(
            P("feat", None),
            P(None, "feat"),
            P("feat"),
            P("tgt", "feat", None),
            P("tgt", None),
            P("tgt", "feat", None),
        ),
        out_specs=(
            P(None, ("feat", "tgt")),
            P(("feat", "tgt")),
            P("tgt", "feat", None),
            P("tgt", None),
        ),
        check_vma=False,
    )
```

profile of v0, /device:TPU:1, one launch (start us, length us, event | category | flops | bytes accessed | tf_op | source)
XLA Modules:
  0.0 1493.3 jit_solution(6703649330818770816)
XLA Ops:
  7.2 0.0 copy-start
  7.2 0.0 copy-start.4
  7.2 0.0 all-gather.5.cloned.1.call-start
  7.2 0.7 all-gather.5.cloned.1.call-update
  7.9 0.0 all-reduce.3.cloned.1.call-start
  8.0 310.1 %all-gather.5.cloned.1.call-done = bf16[64,3,4096]{2,1,0:T(4,128)(2,1)} async-done(((bf16[1,3,4096]{2,1,0:T(4,128)(2,1)}), bf16[64,3,4096]{2,1,0:T(4,128)(2,1)}) %all-gather.5.cloned.1.call-update) | async-done | bytes 1572880 | tf_op jit(solution)/shard_map/all_gather | solution.py:8
  318.0 4.3 reshape.13
  322.3 0.0 copy-done.4
  322.3 2.6 fusion.7
  325.0 0.0 copy-done
  325.0 2.2 fusion.2
  327.2 0.0 copy-start.5
  327.2 0.0 copy-start.2
  327.2 0.0 copy-start.3
  327.2 0.0 all-reduce.3.cloned.1.call-update
  327.3 0.0 all-gather.7.cloned.1.call-start
  327.3 0.6 copy-done.5
  327.9 0.6 dynamic-slice
  329.1 716.0 %all-reduce.3.cloned.1.call-done = f32[192,4096]{1,0:T(8,128)} async-done(((f32[192,4096]{1,0:T(8,128)}), f32[192,4096]{1,0:T(8,128)}) %all-reduce.3.cloned.1.call-update) | async-done | bytes 3145744
  1045.2 0.0 copy-done.2
  1045.2 0.0 copy-done.3
  1045.2 1.6 fusion.10
  1046.8 0.0 all-gather.7.cloned.1.call-update
  1046.8 0.0 reduce-scatter.4.cloned.1.call-start
  1046.9 348.8 %all-gather.7.cloned.1.call-done = bf16[64,3,4096]{2,1,0:T(4,128)(2,1)} async-done(((bf16[1,3,4096]{2,1,0:T(4,128)(2,1)}), bf16[64,3,4096]{2,1,0:T(4,128)(2,1)}) %all-gather.7.cloned.1.call-update) | async-done | bytes 1572880 | tf_op jit(solution)/shard_map/all_gather | solution.py:22
  1395.7 4.3 reshape.15
  1399.9 2.8 fusion.4
  1402.8 0.0 reduce-scatter.4.cloned.1.call-update
  1402.8 0.0 copy-start.1
  1402.8 2.4 convert_reduce_fusion
  1405.2 0.0 copy-done.1
  1405.2 2.8 convolution_bitcast_fusion
  1407.9 74.3 %reduce-scatter.4.cloned.1.call-done = f32[64,192]{1,0:T(8,128)} async-done(((f32[256,192]{1,0:T(8,128)}), f32[64,192]{1,0:T(8,128)}) %reduce-scatter.4.cloned.1.call-update) | async-done | bytes 49168
  1482.3 0.9 copy.15
  1483.2 2.9 convolution_bitcast_fusion.1
  1486.1 0.6 fusion.11
Async XLA Ops:
  7.2 317.8 %copy-start = (bf16[1,256,4096]{2,1,0:T(8,128)(2,1)S(1)}, bf16[1,256,4096]{2,1,0:T(8,128)(2,1)}, u32[]{:S(2)}) copy-start(bf16[1,256,4096]{2,1,0:T(8,128)(2,1)} %param.9) | copy-start | bytes 6291460
  7.2 315.1 %copy-start.4 = (f32[256]{0:T(256)S(1)}, f32[256]{0:T(256)}, u32[]{:S(2)}) copy-start(f32[256]{0:T(256)} %param.8) | copy-start | bytes 3076
  7.2 310.8 %all-gather.5.cloned.1.call-start = ((), (), s32[]{:S(2)}) async-start(), calls=%async_computation.1 | async-start | bytes 2129920 | tf_op jit(solution)/shard_map/all_gather | solution.py:8
  7.9 1037.2 %all-reduce.3.cloned.1.call-start = ((), (), s32[]{:S(2)}) async-start(), calls=%async_computation.4 | async-start | bytes 6291456
  327.2 0.7 copy-start.5
  327.2 717.9 %copy-start.2 = (bf16[1,3,4096]{2,1,0:T(4,128)(2,1)S(1)}, bf16[1,3,4096]{2,1,0:T(4,128)(2,1)}, u32[]{:S(2)}) copy-start(bf16[1,3,4096]{2,1,0:T(4,128)(2,1)} %param.11) | copy-start | bytes 73732
  327.2 717.9 %copy-start.3 = (f32[1,4096]{1,0:T(1,128)S(1)}, f32[1,4096]{1,0:T(1,128)}, u32[]{:S(2)}) copy-start(f32[1,4096]{1,0:T(1,128)} %param.10) | copy-start | bytes 49156
  327.3 1068.4 %all-gather.7.cloned.1.call-start = ((), (), s32[]{:S(2)}) async-start(), calls=%async_computation.2 | async-start | bytes 2129920 | tf_op jit(solution)/shard_map/all_gather | solution.py:22
  1046.8 435.5 %reduce-scatter.4.cloned.1.call-start = ((), (), s32[]{:S(2)}) async-start(), calls=%async_computation.3 | async-start | bytes 327680
  1402.8 2.4 copy-start.1
Sparse Core Ops, SparseCore 0:
  9.8 308.1 all-gather.4
  327.4 717.7 all-reduce.2
  1047.7 347.9 all-gather.6
  1402.9 79.3 reduce-scatter.3
where the time goes:
time: 1490 us
  waiting for transfers between devices  1450 us (97%)
    unnamed x6, waiting for transfers between devices  791 us
    all_gather x1, waiting for transfers between devices, body(): recon_error = lax.all_gather(error_part, 'feat', axis=0, tiled=True)  349 us
    all_gather x1, waiting for transfers between devices, body(): all_rows = lax.all_gather(tokens, 'feat', axis=0, tiled=True)  310 us
  transfers between devices with their start and end apart: 4, of which 4 were waited for; matrix products, arithmetic and copies ran while one was open for 0% of the time, Pallas kernels for 0%

commit v1 on v0

--- a/solution.py
+++ b/solution.py
@@ -19,7 +19,9 @@
         tiled=True,
     )
     error_part = (summed + bias - target.astype(jnp.float32)).astype(jnp.bfloat16)
-    recon_error = lax.all_gather(error_part, "feat", axis=0, tiled=True)
+    recon_error = jnp.concatenate(
+        lax.all_to_all(jnp.stack([error_part] * lax.axis_size("feat")), "feat", 0, 0), axis=0
+    )
     decoder_grads = [
         lax.dot_general(
             feats, recon_error, (((0,), (0,)), ((), ())), preferred_element_type=jnp.float32

time: 1490 us -> 1190 us (0.80)
  waiting for transfers between devices: 1450 us -> 1130 us
    all_gather x1 -> x0, waiting for transfers between devices: 349 us -> none  [body(): recon_error = lax.all_gather(error_part, 'feat', axis=0, tiled=True)]
    all_to_all x0 -> x1, waiting for transfers between devices: none -> 28.6 us  [body(): lax.all_to_all(jnp.stack([error_part] * lax.axis_size('feat')), 'feat', 0...]
    unnamed x6 -> x5, waiting for transfers between devices: 791 us -> 790 us
  transfers between devices with their start and end apart: 4 -> 4, of which waited for: 4 -> 4; matrix products, arithmetic and copies ran while one was open for 0% -> 1% of each run, Pallas kernels for 0% -> 0%
where the time goes in v1:
time: 1190 us; the launch traced here: 1180 us
  waiting for transfers between devices  1130 us (95%)
  matrix products  14.8 us (1%)
  between operations  14.5 us (1%)
  local copies, waits for them, and re-layouts  13.1 us (1%)
    unnamed x5, waiting for transfers between devices  790 us
    all_gather x1, waiting for transfers between devices, body(): all_rows = lax.all_gather(tokens, 'feat', axis=0, tiled=True)  310 us
    all_to_all x1, waiting for transfers between devices, body(): lax.all_to_all(jnp.stack([error_part] * lax.axis_size('feat')), 'feat', 0...  28.6 us
  transfers between devices with their start and end apart: 4, of which 4 were waited for; matrix products, arithmetic and copies ran while one was open for 1% of the time, Pallas kernels for 0%

profile of v1, /device:TPU:1, one launch (start us, length us, event | category | flops | bytes accessed | tf_op | source)
XLA Modules:
  0.0 1184.8 jit_solution(12152591275575421934)
XLA Ops:
  7.2 0.0 copy-start
  7.2 0.0 copy-start.3
  7.2 0.0 all-gather.3.cloned.1.call-start
  7.2 0.7 all-gather.3.cloned.1.call-update
  7.9 0.0 all-reduce.3.cloned.1.call-start
  8.0 310.1 %all-gather.3.cloned.1.call-done = bf16[64,3,4096]{2,1,0:T(4,128)(2,1)} async-done(((bf16[1,3,4096]{2,1,0:T(4,128)(2,1)}), bf16[64,3,4096]{2,1,0:T(4,128)(2,1)}) %all-gather.3.cloned.1.call-update) | async-done | bytes 1572880 | tf_op jit(solution)/shard_map/all_gather | solution.py:8
  318.0 4.3 reshape.19
  322.3 0.0 copy-done.3
  322.3 2.6 fusion.7
  325.0 0.0 copy-done
  325.0 2.2 fusion.2
  327.2 0.0 copy-start.4
  327.2 0.0 copy-start.1
  327.2 0.0 copy-start.2
  327.2 0.0 all-reduce.3.cloned.1.call-update
  327.3 0.6 copy-done.4
  327.9 0.6 dynamic-slice
  329.2 716.0 %all-reduce.3.cloned.1.call-done = f32[192,4096]{1,0:T(8,128)} async-done(((f32[192,4096]{1,0:T(8,128)}), f32[192,4096]{1,0:T(8,128)}) %all-reduce.3.cloned.1.call-update) | async-done | bytes 3145744
  1045.2 0.0 copy-done.1
  1045.2 0.0 copy-done.2
  1045.2 1.0 fusion.8
  1046.2 2.3 stack.6
  1048.5 9.2 all-to-all-start
  1057.7 0.0 reduce-scatter.4.cloned.1.call-start
  1057.7 28.6 %all-to-all-done = bf16[64,3,4096]{2,1,0:T(4,128)(2,1)} async-done(((bf16[64,3,4096]{2,1,0:T(4,128)(2,1)}), bf16[64,3,4096]{2,1,0:T(4,128)(2,1)}, u32[]{:S(2)}, u32[]{:S(2)}) %all-to-all-start) | async-done | bytes 1572896 | tf_op jit(solution)/shard_map/all_to_all | solution.py:23
  1086.3 4.3 reshape.16
  1090.6 2.8 fusion.4
  1093.5 0.0 reduce-scatter.4.cloned.1.call-update
  1093.5 4.2 convolution_bitcast_fusion
  1097.6 3.1 convert_reduce_fusion
  1100.8 73.1 %reduce-scatter.4.cloned.1.call-done = f32[64,192]{1,0:T(8,128)} async-done(((f32[256,192]{1,0:T(8,128)}), f32[64,192]{1,0:T(8,128)}) %reduce-scatter.4.cloned.1.call-update) | async-done | bytes 49168
  1173.9 0.9 copy.15
  1174.8 2.9 convolution_bitcast_fusion.1
  1177.7 0.6 fusion.10
Async XLA Ops:
  7.2 317.8 %copy-start = (bf16[1,256,4096]{2,1,0:T(8,128)(2,1)S(1)}, bf16[1,256,4096]{2,1,0:T(8,128)(2,1)}, u32[]{:S(2)}) copy-start(bf16[1,256,4096]{2,1,0:T(8,128)(2,1)} %param.9) | copy-start | bytes 6291460
  7.2 315.1 %copy-start.3 = (f32[256]{0:T(256)S(1)}, f32[256]{0:T(256)}, u32[]{:S(2)}) copy-start(f32[256]{0:T(256)} %param.8) | copy-start | bytes 3076
  7.2 310.8 %all-gather.3.cloned.1.call-start = ((), (), s32[]{:S(2)}) async-start(), calls=%async_computation.2 | async-start | bytes 2129920 | tf_op jit(solution)/shard_map/all_gather | solution.py:8
  7.9 1037.3 %all-reduce.3.cloned.1.call-start = ((), (), s32[]{:S(2)}) async-start(), calls=%async_computation.4 | async-start | bytes 6291456
  327.2 0.7 copy-start.4
  327.2 717.9 %copy-start.1 = (bf16[1,3,4096]{2,1,0:T(4,128)(2,1)S(1)}, bf16[1,3,4096]{2,1,0:T(4,128)(2,1)}, u32[]{:S(2)}) copy-start(bf16[1,3,4096]{2,1,0:T(4,128)(2,1)} %param.11) | copy-start | bytes 73732
  327.2 717.9 %copy-start.2 = (f32[1,4096]{1,0:T(1,128)S(1)}, f32[1,4096]{1,0:T(1,128)}, u32[]{:S(2)}) copy-start(f32[1,4096]{1,0:T(1,128)} %param.10) | copy-start | bytes 49156
  1048.5 37.8 %all-to-all-start = ((bf16[64,3,4096]{2,1,0:T(4,128)(2,1)}), bf16[64,3,4096]{2,1,0:T(4,128)(2,1)}, u32[]{:S(2)}, u32[]{:S(2)}) async-start(bf16[64,3,4096]{2,1,0:T(4,128)(2,1)} %stack.6), calls=%async_computation | async-start | bytes 4194304 | tf_op jit(solution)/shard_map/all_to_all | solution.py:23
  1057.7 116.2 %reduce-scatter.4.cloned.1.call-start = ((), (), s32[]{:S(2)}) async-start(), calls=%async_computation.3 | async-start | bytes 327680
Sparse Core Ops, SparseCore 0:
  9.8 308.1 all-gather.2
  327.4 717.7 all-reduce.2
  1093.6 80.1 reduce-scatter.3
